TPU v7x, 32 devices: a whole 2x2x4 slice. The times are simulated.
32 devices in a mesh: dp: 4 (over y, x), token: 8 (over z, core).
Axes of the slice: x: 2, y: 2, z: 4, core: 2. Of those that a mesh axis runs over, the one named last changes fastest.
Arguments:
- mix_input: bfloat16 [1536, 8, 768], P('dp', 'token'), may hold values from -6 to 6
- out_grad: bfloat16 [1536, 8, 768], P('dp', 'token'), may hold values from -1.5 to 1.5
- w_up: bfloat16 [8, 768, 3072], P('token'), may hold values from -0.21875 to 0.21875
- w_down: bfloat16 [8, 3072, 768], P('token'), may hold values from -0.109375 to 0.109375
- gain_first: float32 [8, 768], P('token'), may hold values from 0.25 to 1.75
- gain_second: float32 [8, 768], P('token'), may hold values from 0.25 to 1.75
- owner_dev: int32 [8, 1536, 1], P('token', 'dp'), may hold values from 0 to 3; in each aligned block of 384 rows (0 to 383, 384 to 767, ..., all dimensions but the last counted through in order) at most 240 rows name the same one
- slot_row: int32 [8, 1536], P('token', 'dp'), may hold values from 0 to 255
Outputs:
- grad_up: float32 [8, 768, 3072], P('token', 'dp')
- grad_down: float32 [8, 3072, 768], P('token', 'dp')
- row_grad: float32 [8, 1024, 768], P('token', 'dp')
Inputs may be any that keep to these rules, and one draw needn't show every extreme that they name: `owner_dev`: in the rows of one device (aligned blocks of 384 samples of one token) no owner is named by more than 240 rows, a bound that some block reaches.
All inputs are finite; a program needn't handle non-finite values.
Results may differ from a plain program's by a relative error of at most 0.015.
Values may be sent and summed in bfloat16 or wider, within the bound.
A program may use at most 128 MiB of HBM per device.

v0:
```python
import jax
import jax.numpy as jnp
from jax import lax
from jax.sharding import PartitionSpec as P

HOT = 256
EPS = 1e-05
HALF_ROOT = 0.7071067811865476
INV_ROOT_TAU = 0.3989422804014327


def normalize(values):
    center = values - jnp.mean(values, axis=-1, keepdims=True)
    inv_scale = lax.rsqrt(jnp.mean(center * center, axis=-1, keepdims=True) + EPS)
    return (center * inv_scale, inv_scale)


def norm_back(grad_norm, normed, inv_scale):
    mean_grad = jnp.mean(grad_norm, axis=-1, keepdims=True)
    mean_proj = jnp.mean(grad_norm * normed, axis=-1, keepdims=True)
    return inv_scale * (grad_norm - mean_grad - normed * mean_proj)


def gelu_parts(pre_act):
    cumul = 0.5 * (1.0 + jax.scipy.special.erf(pre_act * HALF_ROOT))
    density = jnp.exp(-0.5 * pre_act * pre_act) * INV_ROOT_TAU
    return (pre_act * cumul, cumul + pre_act * density)


def contract_rows(left, right):
    return lax.dot_general(
        left, right, (((0,), (0,)), ((), ())), preferred_element_type=jnp.float32
    )


def contract_cols(left, right):
    return lax.dot_general(
        left, right, (((1,), (1,)), ((), ())), preferred_element_type=jnp.float32
    )


def per_device(mix_input, out_grad, w_up, w_down, gain_first, gain_second, owner_dev, slot_row):
    batch_rows = mix_input.shape[0]
    width = mix_input.shape[2]
    owners = lax.axis_size("dp")
    normed, inv_scale = normalize(mix_input[:, 0, :].astype(jnp.float32))
    hidden_in = (normed * gain_first[0]).astype(jnp.bfloat16)
    pre_act = jnp.dot(hidden_in, w_up[0], preferred_element_type=jnp.float32)
    act_value, act_slope = gelu_parts(pre_act)
    active = act_value.astype(jnp.bfloat16)
    outer_sum = jnp.dot(active, w_down[0], preferred_element_type=jnp.float32) + hidden_in.astype(
        jnp.float32
    )
    normed_out, inv_out = normalize(outer_sum)
    grad_wide = norm_back(
        out_grad[:, 0, :].astype(jnp.float32) * gain_second[0], normed_out, inv_out
    )
    grad_mid = grad_wide.astype(jnp.bfloat16)
    grad_act = contract_cols(grad_mid, w_down[0])
    grad_pre = (grad_act * act_slope).astype(jnp.bfloat16)
    up_whole = contract_rows(hidden_in, grad_pre)
    down_whole = contract_rows(active, grad_mid)
    grad_up, grad_down = (
        lax.psum_scatter(
            up_whole.astype(jnp.bfloat16), "dp", scatter_dimension=0, tiled=True
        ).astype(jnp.float32),
        lax.psum_scatter(
            down_whole.astype(jnp.bfloat16), "dp", scatter_dimension=0, tiled=True
        ).astype(jnp.float32),
    )
    grad_hidden = contract_cols(grad_pre, w_up[0]) + grad_wide
    grad_sum = norm_back(grad_hidden * gain_first[0], normed, inv_scale).astype(jnp.bfloat16)
    pieces = lax.axis_size("token")
    swapped = lax.all_to_all(
        grad_sum.reshape(batch_rows, pieces, width // pieces),
        "token",
        split_axis=1,
        concat_axis=1,
        tiled=True,
    )
    embed_grad = (
        grad_sum.astype(jnp.float32) + swapped.reshape(batch_rows, width).astype(jnp.float32)
    ).astype(jnp.bfloat16)
    owner_ids = owner_dev[0, :, 0]
    slot_ids = slot_row[0]
    capacity = max(2, 8 * (5 * batch_rows // (16 * owners)))
    owner_hot = (
        owner_ids[:, None] == lax.broadcasted_iota(jnp.int32, (batch_rows, owners), 1)
    ).astype(jnp.int32)
    rank_within = jnp.sum((jnp.cumsum(owner_hot, axis=0) - 1) * owner_hot, axis=1)
    place = owner_ids * capacity + rank_within
    dispatch_mask = (
        lax.broadcasted_iota(jnp.int32, (owners * capacity, batch_rows), 0) == place[None, :]
    )
    send_grad = jnp.dot(
        dispatch_mask.astype(jnp.bfloat16), embed_grad, preferred_element_type=jnp.float32
    )
    send_grad = send_grad.astype(jnp.bfloat16).reshape(owners, capacity, width)
    send_slot = jnp.sum(dispatch_mask.astype(jnp.int32) * (slot_ids + 1)[None, :], axis=1) - 1
    send_slot = send_slot.astype(jnp.float32).astype(jnp.bfloat16).reshape(owners, capacity)
    recv_grad, recv_slot = (
        lax.all_to_all(send_grad, "dp", split_axis=0, concat_axis=0, tiled=True),
        lax.all_to_all(send_slot, "dp", split_axis=0, concat_axis=0, tiled=True),
    )
    slot_values = recv_slot.reshape(1, owners * capacity).astype(jnp.float32)
    gather_hot = (
        lax.broadcasted_iota(jnp.int32, (HOT, owners * capacity), 0).astype(jnp.float32)
        == slot_values
    ).astype(jnp.bfloat16)
    row_grad = jnp.dot(
        gather_hot, recv_grad.reshape(owners * capacity, width), preferred_element_type=jnp.float32
    )
    return (grad_up[None], grad_down[None], row_grad[None])


def solution(mesh):
    placed = (
        P("dp", "token", None),
        P("dp", "token", None),
        P("token", None, None),
        P("token", None, None),
        P("token", None),
        P("token", None),
        P("token", "dp", None),
        P("token", "dp"),
    )
    return jax.shard_map(
        per_device,
        mesh=mesh,
        in_specs=placed,
        out_specs=(P("token", "dp", None), P("token", "dp", None), P("token", "dp", None)),
        check_vma=False,
    )
```

profile of v0, /device:TPU:0, one launch (start us, length us, event | category | flops | bytes accessed | tf_op | source)
XLA Modules:
  0.0 167.2 jit_solution(3373217656529832667)
XLA Ops:
  7.2 1.3 convert_reduce_fusion
  8.5 1.4 fusion.36
  10.0 6.4 %multiply_convert_fusion = (bf16[384,3072]{1,0:T(8,128)(2,1)S(1)}, f32[384,3072]{1,0:T(8,128)}) fusion(bf16[1,768,3072]{2,1,0:T(8,128)(2,1)} %param.10, bf16[384,1,768]{2,0,1:T(8,128)(2,1)S(1)} %copy-done, f32[768]{0:T(1024)S(1)} %reduce.1, f32[384]{0:T(512)S(1)} %add_rsqrt_fusion.1, f32[384]{0:T(512)S(1)} %broadcast_multiply_fusion.5), kind=kOutput, calls=%fused_computation.17 | convolution fusion | flops 1819312128 | bytes 12392448 | tf_op jit(solution)/shard_map/dot_general | solution.py:48
  16.4 4.4 %fusion.64 = (f32[384]{0:T(512)S(1)}, f32[384,768]{1,0:T(8,128)S(1)}) fusion(f32[768]{0:T(1024)S(1)} %reduce.1, f32[384]{0:T(512)S(1)} %add_rsqrt_fusion.1, f32[384]{0:T(512)S(1)} %broadcast_multiply_fusion.5, bf16[384,1,768]{2,0,1:T(8,128)(2,1)S(1)} %copy-done, bf16[384,3072]{1,0:T(8,128)(2,1)S(1)} %get-tuple-element.7, bf16[1,3072,768]{2,1,0:T(8,128)(2,1)} %param.11), kind=kOutput, calls=%fused_computation.88 | convolution fusion | flops 1814298240 | bytes 8855040 | tf_op jit(solution)/shard_map/dot_general | solution.py:51
  20.8 0.3 multiply_reduce_fusion
  21.1 0.8 copy-done.1
  21.9 0.4 fusion.42
  22.3 4.7 %convolution_convert_fusion = bf16[3072,768]{1,0:T(8,128)(2,1)} fusion(bf16[384,3072]{1,0:T(8,128)(2,1)S(1)} %get-tuple-element.7, f32[384,768]{1,0:T(8,128)S(1)} %get-tuple-element.10, bf16[384,1,768]{2,0,1:T(8,128)(2,1)S(1)} %copy-done.1, f32[384]{0:T(512)S(1)} %get-tuple-element.12, f32[384]{0:T(512)S(1)} %get-tuple-element.13, f32[768]{0:T(1024)S(1)} %reduce.2, ...), kind=kOutput, calls=%fused_computation.1 | convolution fusion | flops 1816952832 | bytes 8856576 | tf_op jit(solution)/shard_map/dot_general | solution.py:31
  27.0 6.8 %fusion.5 = bf16[384,3072]{1,0:T(8,128)(2,1)S(1)} fusion(f32[384,3072]{1,0:T(8,128)} %get-tuple-element.8, bf16[1,3072,768]{2,1,0:T(8,128)(2,1)} %param.11, f32[384,768]{1,0:T(8,128)S(1)} %get-tuple-element.10, bf16[384,1,768]{2,0,1:T(8,128)(2,1)S(1)} %copy-done.1, f32[384]{0:T(512)S(1)} %get-tuple-element.12, f32[384]{0:T(512)S(1)} %get-tuple-element.13, ...), kind=kOutput, calls=%fused_computation.8 | convolution fusion | flops 1826390016 | bytes 13575168 | tf_op jit(solution)/shard_map/dot_general | solution.py:37
  33.9 1.4 copy-done.6
  35.3 4.7 %convolution_convert_fusion.1 = bf16[768,3072]{1,0:T(8,128)(2,1)} fusion(bf16[384,3072]{1,0:T(8,128)(2,1)S(1)} %fusion.5, bf16[384,1,768]{2,0,1:T(8,128)(2,1)S(1)} %copy-done, f32[768]{0:T(1024)S(1)} %reduce.1, f32[384]{0:T(512)S(1)} %add_rsqrt_fusion.1, f32[384]{0:T(512)S(1)} %broadcast_multiply_fusion.5), kind=kOutput, calls=%fused_computation.2 | convolution fusion | flops 1815773184 | bytes 7673856 | tf_op jit(solution)/shard_map/dot_general | solution.py:31
  40.0 5.5 %fusion.63 = (f32[384]{0:T(512)S(1)}, f32[384]{0:T(512)S(1)}, f32[384,768]{1,0:T(8,128)S(1)}) fusion(f32[384]{0:T(512)S(1)} %add_rsqrt_fusion.1, f32[384]{0:T(512)S(1)} %broadcast_multiply_fusion.5, bf16[384,1,768]{2,0,1:T(8,128)(2,1)S(1)} %copy-done, f32[768]{0:T(1024)S(1)} %reduce.1, f32[384]{0:T(512)S(1)} %get-tuple-element.12, ...), kind=kOutput, calls=%fused_computation.87 | convolution fusion | flops 1816657152 | bytes 10635264 | tf_op jit(solution)/shard_map/dot_general | solution.py:37
  45.5 0.4 fusion.35
  45.9 1.1 copy.17
  47.0 6.6 %all-to-all-start.1 = ((bf16[384,8,96]{0,2,1:T(8,128)(2,1)}), bf16[384,8,96]{0,2,1:T(8,128)(2,1)S(1)}, u32[]{:S(2)}, u32[]{:S(2)}) async-start(bf16[384,8,96]{0,2,1:T(8,128)(2,1)} %bitcast.8), calls=%async_computation.3 | async-start | bytes 1179648 | tf_op jit(solution)/shard_map/all_to_all | solution.py:74
  53.7 1.2 reduce-window.6
  54.9 0.2 slice_reduce_fusion
  55.1 0.2 reduce-window.9
  55.4 0.2 select_reduce_fusion
  55.7 0.7 convert_element_type.137
  56.4 14.0 %all-to-all-done.1 = bf16[384,8,96]{0,2,1:T(8,128)(2,1)S(1)} async-done(((bf16[384,8,96]{0,2,1:T(8,128)(2,1)}), bf16[384,8,96]{0,2,1:T(8,128)(2,1)S(1)}, u32[]{:S(2)}, u32[]{:S(2)}) %all-to-all-start.1) | async-done | bytes 589856 | tf_op jit(solution)/shard_map/all_to_all | solution.py:74
  70.4 3.7 %all-to-all-start = ((bf16[4,1,240]{2,1,0:T(2,128)(2,1)}), bf16[4,1,240]{2,1,0:T(2,128)(2,1)S(1)}, u32[]{:S(2)}, u32[]{:S(2)}) async-start(bf16[4,1,240]{2,1,0:T(2,128)(2,1)} %convert_element_type.137), calls=%async_computation.2 | async-start | bytes 8192 | tf_op jit(solution)/shard_map/all_to_all | solution.py:103
  74.1 0.1 bitcast_convert_fusion.2
  74.2 0.4 copy.18
  74.6 2.1 %convolution_convert_fusion.2 = bf16[960,768]{1,0:T(8,128)(2,1)} fusion(s32[384]{0:T(512)S(1)} %multiply_add_fusion, f32[384,768]{1,0:T(8,128)S(1)} %copy.18, bf16[384,768]{1,0:T(8,128)(2,1)S(1)} %fusion.35), kind=kOutput, calls=%fused_computation.22 | convolution fusion | flops 568221696 | bytes 3245568 | tf_op jit(solution)/shard_map/dot_general | solution.py:95
  76.7 2.2 %all-to-all-done = bf16[4,1,240]{2,1,0:T(2,128)(2,1)S(1)} async-done(((bf16[4,1,240]{2,1,0:T(2,128)(2,1)}), bf16[4,1,240]{2,1,0:T(2,128)(2,1)S(1)}, u32[]{:S(2)}, u32[]{:S(2)}) %all-to-all-start) | async-done | bytes 1952 | tf_op jit(solution)/shard_map/all_to_all | solution.py:103
  78.9 3.6 %all-to-all-start.2 = ((bf16[4,240,768]{2,1,0:T(8,128)(2,1)}), bf16[4,240,768]{2,1,0:T(8,128)(2,1)S(1)}, u32[]{:S(2)}, u32[]{:S(2)}) async-start(bf16[4,240,768]{2,1,0:T(8,128)(2,1)} %bitcast.10), calls=%async_computation.4 | async-start | bytes 2949120 | tf_op jit(solution)/shard_map/all_to_all | solution.py:102
  82.6 18.5 %all-to-all-done.2 = bf16[4,240,768]{2,1,0:T(8,128)(2,1)S(1)} async-done(((bf16[4,240,768]{2,1,0:T(8,128)(2,1)}), bf16[4,240,768]{2,1,0:T(8,128)(2,1)S(1)}, u32[]{:S(2)}, u32[]{:S(2)}) %all-to-all-start.2) | async-done | bytes 1474592 | tf_op jit(solution)/shard_map/all_to_all | solution.py:102
  101.1 1.5 convolution_bitcast_fusion
  102.6 2.8 %bitcast_convert_fusion = f32[1,768,768]{2,1,0:T(8,128)} fusion(bf16[768,768]{1,0:T(8,128)(2,1)} %reduce-scatter.5.cloned.1.call-done), kind=kLoop, calls=%fused_computation.44 | loop fusion | flops 589824 | bytes 3538944 | tf_op jit(solution)/shard_map/broadcast_in_dim | solution.py:113
  105.5 52.0 %reduce-scatter.3.cloned.1.call-done = bf16[192,3072]{1,0:T(8,128)(2,1)} async-done(((bf16[768,3072]{1,0:T(8,128)(2,1)}), bf16[192,3072]{1,0:T(8,128)(2,1)}) %reduce-scatter.3.cloned.1.call-update) | async-done | bytes 1179664 | tf_op jit(solution)/shard_map/reduce_scatter | solution.py:64
  157.5 2.9 %bitcast_convert_fusion.1 = f32[1,192,3072]{2,1,0:T(8,128)} fusion(bf16[192,3072]{1,0:T(8,128)(2,1)} %reduce-scatter.3.cloned.1.call-done), kind=kLoop, calls=%fused_computation.45 | loop fusion | flops 589824 | bytes 3538944 | tf_op jit(solution)/shard_map/broadcast_in_dim | solution.py:113
  (36 shorter events, 0.5 us)
Async XLA Ops:
  7.2 2.8 %copy-start = (bf16[384,1,768]{2,0,1:T(8,128)(2,1)S(1)}, bf16[384,1,768]{2,0,1:T(8,128)(2,1)}, u32[]{:S(2)}) copy-start(bf16[384,1,768]{2,0,1:T(8,128)(2,1)} %param.8) | copy-start | bytes 1769476
  7.2 2.7 %copy-start.2 = (f32[1,768]{1,0:T(1,128)S(1)}, f32[1,768]{1,0:T(1,128)}, u32[]{:S(2)}) copy-start(f32[1,768]{1,0:T(1,128)} %param.12) | copy-start | bytes 9220
  7.2 2.7 %copy-start.3 = (f32[1,768]{1,0:T(1,128)S(1)}, f32[1,768]{1,0:T(1,128)}, u32[]{:S(2)}) copy-start(f32[1,768]{1,0:T(1,128)} %param.13) | copy-start | bytes 9220
  7.2 95.4 %reduce-scatter.5.cloned.1.call-start = ((), (), s32[]{:S(2)}) async-start(), calls=%async_computation.6 | async-start | bytes 5898240 | tf_op jit(solution)/shard_map/reduce_scatter | solution.py:67
  20.8 1.1 copy-start.1
  27.0 130.5 %reduce-scatter.3.cloned.1.call-start = ((), (), s32[]{:S(2)}) async-start(), calls=%async_computation.5 | async-start | bytes 5898240 | tf_op jit(solution)/shard_map/reduce_scatter | solution.py:64
  33.9 1.4 copy-start.6
  45.9 7.7 %copy-start.5 = (s32[1,384,1]{1,2,0:T(1,128)S(1)}, s32[1,384,1]{1,2,0:T(1,128)}, u32[]{:S(2)}) copy-start(s32[1,384,1]{1,2,0:T(1,128)} %param.14) | copy-start | bytes 4612
  45.9 9.4 %copy-start.4 = (s32[1,384]{1,0:T(1,128)S(1)}, s32[1,384]{1,0:T(1,128)}, u32[]{:S(2)}) copy-start(s32[1,384]{1,0:T(1,128)} %param.15) | copy-start | bytes 4612
  47.0 23.4 %all-to-all-start.1 = ((bf16[384,8,96]{0,2,1:T(8,128)(2,1)}), bf16[384,8,96]{0,2,1:T(8,128)(2,1)S(1)}, u32[]{:S(2)}, u32[]{:S(2)}) async-start(bf16[384,8,96]{0,2,1:T(8,128)(2,1)} %bitcast.8), calls=%async_computation.3 | async-start | bytes 1179648 | tf_op jit(solution)/shard_map/all_to_all | solution.py:74
  70.4 8.5 %all-to-all-start = ((bf16[4,1,240]{2,1,0:T(2,128)(2,1)}), bf16[4,1,240]{2,1,0:T(2,128)(2,1)S(1)}, u32[]{:S(2)}, u32[]{:S(2)}) async-start(bf16[4,1,240]{2,1,0:T(2,128)(2,1)} %convert_element_type.137), calls=%async_computation.2 | async-start | bytes 8192 | tf_op jit(solution)/shard_map/all_to_all | solution.py:103
  78.9 22.2 %all-to-all-start.2 = ((bf16[4,240,768]{2,1,0:T(8,128)(2,1)}), bf16[4,240,768]{2,1,0:T(8,128)(2,1)S(1)}, u32[]{:S(2)}, u32[]{:S(2)}) async-start(bf16[4,240,768]{2,1,0:T(8,128)(2,1)} %bitcast.10), calls=%async_computation.4 | async-start | bytes 2949120 | tf_op jit(solution)/shard_map/all_to_all | solution.py:102
Sparse Core Ops, SparseCore 0:
  27.1 68.5 reduce-scatter.4
  98.7 58.7 reduce-scatter.2
where the time goes:
time: 168 us; the launch traced here: 167 us
  waiting for transfers between devices  86.8 us (52%)
  matrix products  36.1 us (21%)
  between operations  14.2 us (8%)
  starting transfers between devices  14 us (8%)
  other arithmetic  11.5 us (7%)
  local copies, waits for them, and re-layouts  4.61 us (3%)
    reduce_scatter x1, waiting for transfers between devices, per_device(): lax.psum_scatter(up_whole.astype(jnp.bfloat16), 'dp', scatter_dimension=0...  52 us
    all_to_all x1, waiting for transfers between devices, per_device(): lax.all_to_all(send_grad, 'dp', split_axis=0, concat_axis=0, tiled=True)  18.5 us
    all_to_all x1, waiting for transfers between devices, per_device(): lax.all_to_all(grad_sum.reshape(batch_rows, pieces, width // pieces), 'to...  14 us
    dot_general x2, matrix products, contract_cols(): lax.dot_general(left, right, (((1,), (1,)), ((), ())), preferred_element_...  12.3 us
    dot_general x2, matrix products, contract_rows(): lax.dot_general(left, right, (((0,), (0,)), ((), ())), preferred_element_...  9.4 us
    all_to_all x1, starting transfers between devices, per_device(): lax.all_to_all(grad_sum.reshape(batch_rows, pieces, width // pieces), 'to...  6.64 us
    dot_general x1, matrix products, per_device(): pre_act = jnp.dot(hidden_in, w_up[0], preferred_element_type=jnp.float32)  6.38 us
    broadcast_in_dim x2, other arithmetic, per_device(): return (grad_up[None], grad_down[None], row_grad[None])  5.78 us
  transfers between devices with their start and end apart: 5, of which 4 were waited for; matrix products, arithmetic and copies ran while one was open for 17% of the time, Pallas kernels for 0%

commit v1 on v0

--- a/solution.py
+++ b/solution.py
@@ -1,3 +1,4 @@
+import functools
 import jax
 import jax.numpy as jnp
 from jax import lax
@@ -7,6 +8,21 @@
 EPS = 1e-05
 HALF_ROOT = 0.7071067811865476
 INV_ROOT_TAU = 0.3989422804014327
+
+
+def side_press(panel, pos_dim, d0):
+    return jnp.concatenate(
+        jax.lax.all_to_all(
+            jnp.stack(jnp.split(panel, jax.lax.axis_size("token"), axis=pos_dim)),
+            axis_name="token",
+            split_axis=0,
+            concat_axis=0,
+        ),
+        axis=d0,
+    )
+
+
+recast_pieces_all = functools.partial(side_press, pos_dim=1, d0=1)
 
 
 def normalize(values):
@@ -71,13 +87,7 @@
     grad_hidden = contract_cols(grad_pre, w_up[0]) + grad_wide
     grad_sum = norm_back(grad_hidden * gain_first[0], normed, inv_scale).astype(jnp.bfloat16)
     pieces = lax.axis_size("token")
-    swapped = lax.all_to_all(
-        grad_sum.reshape(batch_rows, pieces, width // pieces),
-        "token",
-        split_axis=1,
-        concat_axis=1,
-        tiled=True,
-    )
+    swapped = recast_pieces_all(grad_sum.reshape(batch_rows, pieces, width // pieces))
     embed_grad = (
         grad_sum.astype(jnp.float32) + swapped.reshape(batch_rows, width).astype(jnp.float32)
     ).astype(jnp.bfloat16)

time: 168 us -> 161 us (0.958)
  waiting for transfers between devices: 86.8 us -> 75.5 us
  local copies, waits for them, and re-layouts: 4.61 us -> 8.97 us
    reduce_scatter x1, waiting for transfers between devices: 52 us -> 34.7 us  [per_device(): lax.psum_scatter(up_whole.astype(jnp.bfloat16), 'dp', scatter_dimension=0...]
    all_to_all x1, waiting for transfers between devices: 18.5 us -> 24.5 us  [per_device(): lax.all_to_all(send_grad, 'dp', split_axis=0, concat_axis=0, tiled=True)]
    unnamed x14 -> x21, local copies, waits for them, and re-layouts: 2.21 us -> 6.69 us
  transfers between devices with their start and end apart: 5 -> 5, of which waited for: 4 -> 4; matrix products, arithmetic and copies ran while one was open for 17% -> 20% of each run, Pallas kernels for 0% -> 0%
where the time goes in v1:
time: 161 us; the launch traced here: 160 us
  waiting for transfers between devices  75.5 us (47%)
  matrix products  36.1 us (22%)
  between operations  14.2 us (9%)
  starting transfers between devices  14 us (9%)
  other arithmetic  11.4 us (7%)
  local copies, waits for them, and re-layouts  8.97 us (6%)
    reduce_scatter x1, waiting for transfers between devices, per_device(): lax.psum_scatter(up_whole.astype(jnp.bfloat16), 'dp', scatter_dimension=0...  34.7 us
    all_to_all x1, waiting for transfers between devices, per_device(): lax.all_to_all(send_grad, 'dp', split_axis=0, concat_axis=0, tiled=True)  24.5 us
    all_to_all x1, waiting for transfers between devices, side_press(): jax.lax.all_to_all(jnp.stack(jnp.split(panel, jax.lax.axis_size('token'),...  14 us
    dot_general x2, matrix products, contract_cols(): lax.dot_general(left, right, (((1,), (1,)), ((), ())), preferred_element_...  12.3 us
    dot_general x2, matrix products, contract_rows(): lax.dot_general(left, right, (((0,), (0,)), ((), ())), preferred_element_...  9.4 us
    unnamed x21, local copies, waits for them, and re-layouts  6.69 us
    all_to_all x1, starting transfers between devices, side_press(): jax.lax.all_to_all(jnp.stack(jnp.split(panel, jax.lax.axis_size('token'),...  6.64 us
    dot_general x1, matrix products, per_device(): pre_act = jnp.dot(hidden_in, w_up[0], preferred_element_type=jnp.float32)  6.38 us
  transfers between devices with their start and end apart: 5, of which 4 were waited for; matrix products, arithmetic and copies ran while one was open for 20% of the time, Pallas kernels for 0%

profile of v1, /device:TPU:0, one launch (start us, length us, event | category | flops | bytes accessed | tf_op | source)
XLA Modules:
  0.0 160.3 jit_solution(14971728084430291873)
XLA Ops:
  7.2 1.3 convert_reduce_fusion
  8.5 1.4 fusion.36
  10.0 6.4 %multiply_convert_fusion = (bf16[384,3072]{1,0:T(8,128)(2,1)S(1)}, f32[384,3072]{1,0:T(8,128)}) fusion(bf16[1,768,3072]{2,1,0:T(8,128)(2,1)} %param.10, bf16[384,1,768]{2,0,1:T(8,128)(2,1)S(1)} %copy-done, f32[768]{0:T(1024)S(1)} %reduce.1, f32[384]{0:T(512)S(1)} %add_rsqrt_fusion.1, f32[384]{0:T(512)S(1)} %broadcast_multiply_fusion.5), kind=kOutput, calls=%fused_computation.17 | convolution fusion | flops 1819312128 | bytes 12392448 | tf_op jit(solution)/shard_map/dot_general | solution.py:64
  16.4 4.4 %fusion.72 = (f32[384]{0:T(512)S(1)}, f32[384,768]{1,0:T(8,128)S(1)}) fusion(f32[768]{0:T(1024)S(1)} %reduce.1, f32[384]{0:T(512)S(1)} %add_rsqrt_fusion.1, f32[384]{0:T(512)S(1)} %broadcast_multiply_fusion.5, bf16[384,1,768]{2,0,1:T(8,128)(2,1)S(1)} %copy-done, bf16[384,3072]{1,0:T(8,128)(2,1)S(1)} %get-tuple-element.7, bf16[1,3072,768]{2,1,0:T(8,128)(2,1)} %param.11), kind=kOutput, calls=%fused_computation.103 | convolution fusion | flops 1814298240 | bytes 8855040 | tf_op jit(solution)/shard_map/dot_general | solution.py:67
  21.1 0.8 copy-done.1
  21.9 0.4 fusion.42
  22.3 4.7 %convolution_convert_fusion = bf16[3072,768]{1,0:T(8,128)(2,1)} fusion(bf16[384,3072]{1,0:T(8,128)(2,1)S(1)} %get-tuple-element.7, f32[384,768]{1,0:T(8,128)S(1)} %get-tuple-element.10, bf16[384,1,768]{2,0,1:T(8,128)(2,1)S(1)} %copy-done.1, f32[384]{0:T(512)S(1)} %get-tuple-element.12, f32[384]{0:T(512)S(1)} %get-tuple-element.13, f32[768]{0:T(1024)S(1)} %reduce.2, ...), kind=kOutput, calls=%fused_computation.1 | convolution fusion | flops 1816952832 | bytes 8856576 | tf_op jit(solution)/shard_map/dot_general | solution.py:47
  27.0 6.8 %fusion.5 = bf16[384,3072]{1,0:T(8,128)(2,1)S(1)} fusion(f32[384,3072]{1,0:T(8,128)} %get-tuple-element.8, bf16[1,3072,768]{2,1,0:T(8,128)(2,1)} %param.11, f32[384,768]{1,0:T(8,128)S(1)} %get-tuple-element.10, bf16[384,1,768]{2,0,1:T(8,128)(2,1)S(1)} %copy-done.1, f32[384]{0:T(512)S(1)} %get-tuple-element.12, f32[384]{0:T(512)S(1)} %get-tuple-element.13, ...), kind=kOutput, calls=%fused_computation.8 | convolution fusion | flops 1826390016 | bytes 13575168 | tf_op jit(solution)/shard_map/dot_general | solution.py:53
  33.9 1.4 copy-done.6
  35.3 4.7 %convolution_convert_fusion.1 = bf16[768,3072]{1,0:T(8,128)(2,1)} fusion(bf16[384,3072]{1,0:T(8,128)(2,1)S(1)} %fusion.5, bf16[384,1,768]{2,0,1:T(8,128)(2,1)S(1)} %copy-done, f32[768]{0:T(1024)S(1)} %reduce.1, f32[384]{0:T(512)S(1)} %add_rsqrt_fusion.1, f32[384]{0:T(512)S(1)} %broadcast_multiply_fusion.5), kind=kOutput, calls=%fused_computation.2 | convolution fusion | flops 1815773184 | bytes 7673856 | tf_op jit(solution)/shard_map/dot_general | solution.py:47
  40.0 5.5 %fusion.71 = (f32[384]{0:T(512)S(1)}, f32[384]{0:T(512)S(1)}, f32[384,768]{1,0:T(8,128)S(1)}) fusion(f32[384]{0:T(512)S(1)} %add_rsqrt_fusion.1, f32[384]{0:T(512)S(1)} %broadcast_multiply_fusion.5, bf16[384,1,768]{2,0,1:T(8,128)(2,1)S(1)} %copy-done, f32[768]{0:T(1024)S(1)} %reduce.1, f32[384]{0:T(512)S(1)} %get-tuple-element.12, ...), kind=kOutput, calls=%fused_computation.102 | convolution fusion | flops 1816657152 | bytes 10635264 | tf_op jit(solution)/shard_map/dot_general | solution.py:53
  46.2 0.6 fusion.64
  46.9 0.6 fusion.63
  47.5 0.6 fusion.62
  48.2 0.6 fusion.61
  48.8 0.6 fusion.60
  49.4 0.6 fusion.59
  50.1 0.6 fusion.58
  50.7 0.6 fusion.57
  51.4 6.6 %all-to-all-start.1 = ((bf16[8,384,1,96]{1,3,2,0:T(8,128)(2,1)}), bf16[8,384,1,96]{1,3,2,0:T(8,128)(2,1)S(1)}, u32[]{:S(2)}, u32[]{:S(2)}) async-start(bf16[8,384,1,96]{1,3,2,0:T(8,128)(2,1)} %fusion.57), calls=%async_computation.3 | async-start | bytes 1179648 | tf_op jit(solution)/shard_map/all_to_all | solution.py:15
  58.0 1.2 reduce-window.6
  60.0 0.7 convert_element_type.142
  60.7 14.0 %all-to-all-done.1 = bf16[8,384,1,96]{1,3,2,0:T(8,128)(2,1)S(1)} async-done(((bf16[8,384,1,96]{1,3,2,0:T(8,128)(2,1)}), bf16[8,384,1,96]{1,3,2,0:T(8,128)(2,1)S(1)}, u32[]{:S(2)}, u32[]{:S(2)}) %all-to-all-start.1) | async-done | bytes 589856 | tf_op jit(solution)/shard_map/all_to_all | solution.py:15
  74.7 3.7 %all-to-all-start = ((bf16[4,1,240]{2,1,0:T(2,128)(2,1)}), bf16[4,1,240]{2,1,0:T(2,128)(2,1)S(1)}, u32[]{:S(2)}, u32[]{:S(2)}) async-start(bf16[4,1,240]{2,1,0:T(2,128)(2,1)} %convert_element_type.142), calls=%async_computation.2 | async-start | bytes 8192 | tf_op jit(solution)/shard_map/all_to_all | solution.py:113
  78.9 2.1 %convolution_convert_fusion.2 = bf16[960,768]{1,0:T(8,128)(2,1)} fusion(s32[384]{0:T(512)S(1)} %multiply_add_fusion, f32[384,768]{1,0:T(8,128)S(1)} %copy.26, bf16[384,768]{1,0:T(8,128)(2,1)S(1)} %fusion.35), kind=kOutput, calls=%fused_computation.22 | convolution fusion | flops 568221696 | bytes 3245568 | tf_op jit(solution)/shard_map/dot_general | solution.py:105
  81.0 2.3 %all-to-all-done = bf16[4,1,240]{2,1,0:T(2,128)(2,1)S(1)} async-done(((bf16[4,1,240]{2,1,0:T(2,128)(2,1)}), bf16[4,1,240]{2,1,0:T(2,128)(2,1)S(1)}, u32[]{:S(2)}, u32[]{:S(2)}) %all-to-all-start) | async-done | bytes 1952 | tf_op jit(solution)/shard_map/all_to_all | solution.py:113
  83.3 3.6 %all-to-all-start.2 = ((bf16[4,240,768]{2,1,0:T(8,128)(2,1)}), bf16[4,240,768]{2,1,0:T(8,128)(2,1)S(1)}, u32[]{:S(2)}, u32[]{:S(2)}) async-start(bf16[4,240,768]{2,1,0:T(8,128)(2,1)} %bitcast.19), calls=%async_computation.4 | async-start | bytes 2949120 | tf_op jit(solution)/shard_map/all_to_all | solution.py:112
  87.0 24.5 %all-to-all-done.2 = bf16[4,240,768]{2,1,0:T(8,128)(2,1)S(1)} async-done(((bf16[4,240,768]{2,1,0:T(8,128)(2,1)}), bf16[4,240,768]{2,1,0:T(8,128)(2,1)S(1)}, u32[]{:S(2)}, u32[]{:S(2)}) %all-to-all-start.2) | async-done | bytes 1474592 | tf_op jit(solution)/shard_map/all_to_all | solution.py:112
  111.5 1.5 convolution_bitcast_fusion
  113.0 2.8 %bitcast_convert_fusion = f32[1,768,768]{2,1,0:T(8,128)} fusion(bf16[768,768]{1,0:T(8,128)(2,1)} %reduce-scatter.5.cloned.1.call-done), kind=kLoop, calls=%fused_computation.44 | loop fusion | flops 589824 | bytes 3538944 | tf_op jit(solution)/shard_map/broadcast_in_dim | solution.py:123
  115.8 34.7 %reduce-scatter.3.cloned.1.call-done = bf16[192,3072]{1,0:T(8,128)(2,1)} async-done(((bf16[768,3072]{1,0:T(8,128)(2,1)}), bf16[192,3072]{1,0:T(8,128)(2,1)}) %reduce-scatter.3.cloned.1.call-update) | async-done | bytes 1179664 | tf_op jit(solution)/shard_map/reduce_scatter | solution.py:80
  150.5 2.9 %bitcast_convert_fusion.1 = f32[1,192,3072]{2,1,0:T(8,128)} fusion(bf16[192,3072]{1,0:T(8,128)(2,1)} %reduce-scatter.3.cloned.1.call-done), kind=kLoop, calls=%fused_computation.45 | loop fusion | flops 589824 | bytes 3538944 | tf_op jit(solution)/shard_map/broadcast_in_dim | solution.py:123
  (44 shorter events, 2.5 us)
Async XLA Ops:
  7.2 2.8 %copy-start = (bf16[384,1,768]{2,0,1:T(8,128)(2,1)S(1)}, bf16[384,1,768]{2,0,1:T(8,128)(2,1)}, u32[]{:S(2)}) copy-start(bf16[384,1,768]{2,0,1:T(8,128)(2,1)} %param.8) | copy-start | bytes 1769476
  7.2 2.7 %copy-start.2 = (f32[1,768]{1,0:T(1,128)S(1)}, f32[1,768]{1,0:T(1,128)}, u32[]{:S(2)}) copy-start(f32[1,768]{1,0:T(1,128)} %param.12) | copy-start | bytes 9220
  7.2 2.7 %copy-start.3 = (f32[1,768]{1,0:T(1,128)S(1)}, f32[1,768]{1,0:T(1,128)}, u32[]{:S(2)}) copy-start(f32[1,768]{1,0:T(1,128)} %param.13) | copy-start | bytes 9220
  7.2 105.8 %reduce-scatter.5.cloned.1.call-start = ((), (), s32[]{:S(2)}) async-start(), calls=%async_computation.6 | async-start | bytes 5898240 | tf_op jit(solution)/shard_map/reduce_scatter | solution.py:83
  20.8 1.1 copy-start.1
  27.0 123.5 %reduce-scatter.3.cloned.1.call-start = ((), (), s32[]{:S(2)}) async-start(), calls=%async_computation.5 | async-start | bytes 5898240 | tf_op jit(solution)/shard_map/reduce_scatter | solution.py:80
  33.9 1.4 copy-start.6
  46.2 11.8 %copy-start.5 = (s32[1,384,1]{1,2,0:T(1,128)S(1)}, s32[1,384,1]{1,2,0:T(1,128)}, u32[]{:S(2)}) copy-start(s32[1,384,1]{1,2,0:T(1,128)} %param.14) | copy-start | bytes 4612
  46.2 13.4 %copy-start.4 = (s32[1,384]{1,0:T(1,128)S(1)}, s32[1,384]{1,0:T(1,128)}, u32[]{:S(2)}) copy-start(s32[1,384]{1,0:T(1,128)} %param.15) | copy-start | bytes 4612
  51.4 23.4 %all-to-all-start.1 = ((bf16[8,384,1,96]{1,3,2,0:T(8,128)(2,1)}), bf16[8,384,1,96]{1,3,2,0:T(8,128)(2,1)S(1)}, u32[]{:S(2)}, u32[]{:S(2)}) async-start(bf16[8,384,1,96]{1,3,2,0:T(8,128)(2,1)} %fusion.57), calls=%async_computation.3 | async-start | bytes 1179648 | tf_op jit(solution)/shard_map/all_to_all | solution.py:15
  74.7 8.5 %all-to-all-start = ((bf16[4,1,240]{2,1,0:T(2,128)(2,1)}), bf16[4,1,240]{2,1,0:T(2,128)(2,1)S(1)}, u32[]{:S(2)}, u32[]{:S(2)}) async-start(bf16[4,1,240]{2,1,0:T(2,128)(2,1)} %convert_element_type.142), calls=%async_computation.2 | async-start | bytes 8192 | tf_op jit(solution)/shard_map/all_to_all | solution.py:113
  83.3 28.2 %all-to-all-start.2 = ((bf16[4,240,768]{2,1,0:T(8,128)(2,1)}), bf16[4,240,768]{2,1,0:T(8,128)(2,1)S(1)}, u32[]{:S(2)}, u32[]{:S(2)}) async-start(bf16[4,240,768]{2,1,0:T(8,128)(2,1)} %bitcast.19), calls=%async_computation.4 | async-start | bytes 2949120 | tf_op jit(solution)/shard_map/all_to_all | solution.py:112
Sparse Core Ops, SparseCore 0:
  27.1 59.7 reduce-scatter.4
  89.9 60.5 reduce-scatter.2
